TPU v7x, 32 devices: a whole 2x2x4 slice. The times are simulated.
32 devices in a mesh: dp: 4 (over x, core), fsdp: 2 (over y), tensor: 4 (over z).
Axes of the slice: x: 2, y: 2, z: 4, core: 2. Of those that a mesh axis runs over, the one named last changes fastest.
Arguments:
- layer_input: bfloat16 [4096, 2048], P(('dp', 'fsdp', 'tensor')), may hold values from -6 to 6
- first_gain: bfloat16 [2048], P('fsdp'), may hold values from 0.5 to 1.5
- w_query: bfloat16 [2048, 2048], P('fsdp', 'tensor'), may hold values from -0.125 to 0.125
- w_key: bfloat16 [2048, 2048], P('fsdp', 'tensor'), may hold values from -0.125 to 0.125
- w_value: bfloat16 [2048, 2048], P('fsdp', 'tensor'), may hold values from -0.125 to 0.125
- w_gating: bfloat16 [2048, 2048], P('fsdp', 'tensor'), may hold values from -0.125 to 0.125
- w_beta: bfloat16 [2048, 16], P('fsdp', 'tensor'), may hold values from -0.125 to 0.125
- conv_query: bfloat16 [4, 2048], P(None, 'tensor'), may hold values from -3 to 3
- conv_key: bfloat16 [4, 2048], P(None, 'tensor'), may hold values from -3 to 3
- conv_value: bfloat16 [4, 2048], P(None, 'tensor'), may hold values from -3 to 3
- head_gain: bfloat16 [128], replicated, may hold values from 0.5 to 1.5
- w_project: bfloat16 [2048, 2048], P('tensor', 'fsdp'), may hold values from -0.1875 to 0.1875
- second_gain: bfloat16 [2048], P('fsdp'), may hold values from 0.5 to 1.5
- w_gate: bfloat16 [2048, 5632], P('fsdp', 'tensor'), may hold values from -0.125 to 0.125
- w_up: bfloat16 [2048, 5632], P('fsdp', 'tensor'), may hold values from -0.125 to 0.125
- w_down: bfloat16 [5632, 2048], P('tensor', 'fsdp'), may hold values from -0.109375 to 0.109375
- doc_starts: int32 [8, 4], P(('dp', 'fsdp')), may hold values from 1 to 508, as said below
- seq_lengths: int32 [8], P(('dp', 'fsdp')), may hold values from 256 to 512, as said below
- output_grad: bfloat16 [4096, 2048], P(('dp', 'fsdp', 'tensor')), may hold values from -6 to 6
Outputs:
- result: bfloat16 [4096, 2048], P(('dp', 'fsdp', 'tensor'))
- input_grad: float32 [4096, 2048], P(('dp', 'fsdp', 'tensor'))
- grad_first: float32 [2048], P(('dp', 'fsdp'))
- grad_query: float32 [2048, 2048], P(('dp', 'fsdp'), 'tensor')
- grad_key: float32 [2048, 2048], P(('dp', 'fsdp'), 'tensor')
- grad_value: float32 [2048, 2048], P(('dp', 'fsdp'), 'tensor')
- grad_gating: float32 [2048, 2048], P(('dp', 'fsdp'), 'tensor')
- grad_beta: float32 [2048, 16], P(('dp', 'fsdp'), 'tensor')
- convgrad_query: float32 [4, 2048], P(None, 'tensor')
- convgrad_key: float32 [4, 2048], P(None, 'tensor')
- convgrad_value: float32 [4, 2048], P(None, 'tensor')
- grad_head: float32 [128], replicated
- grad_project: float32 [2048, 2048], P('tensor', ('dp', 'fsdp'))
- grad_second: float32 [2048], P(('dp', 'fsdp'))
- grad_gate: float32 [2048, 5632], P(('dp', 'fsdp'), 'tensor')
- grad_up: float32 [2048, 5632], P(('dp', 'fsdp'), 'tensor')
- grad_down: float32 [5632, 2048], P('tensor', ('dp', 'fsdp'))
Inputs may be any that keep to these rules, and one draw needn't show every extreme that they name: `doc_starts`: each row rises strictly; position 0 begins the first document of a sequence and each entry begins the next. `seq_lengths`: rows at positions at or past a sequence's length are padding.
All inputs are finite; a program needn't handle non-finite values.
Results may differ from a plain program's by a relative error of at most 0.015.
Values may be sent and summed in bfloat16 or wider, within the bound.
A program may use at most 256 MiB of HBM per device.

v0:
```python
import jax
import jax.numpy as jnp
from jax import lax
from jax.sharding import PartitionSpec as P

KERNEL = 4
BLOCK = 64


def rms_scale(values):
    return lax.rsqrt(jnp.mean(values * values, axis=-1, keepdims=True) + 1e-05)


def rms_back(values, scale_rows, gain, grad):
    scaled_grad = grad * gain
    inner = jnp.mean(scaled_grad * values, axis=-1, keepdims=True)
    return scale_rows * (scaled_grad - values * scale_rows * scale_rows * inner)


def short_conv(raw_rows, weights, doc_ids):
    row_count = raw_rows.shape[0]
    total = jnp.zeros_like(raw_rows)
    for tap_index in range(KERNEL):
        delay_rows = KERNEL - 1 - tap_index
        moved = jnp.pad(raw_rows, ((delay_rows, 0), (0, 0)))[:row_count]
        moved_doc = jnp.pad(doc_ids, (delay_rows, 0), constant_values=-1)[:row_count]
        keep_mask = (moved_doc == doc_ids).astype(raw_rows.dtype)
        total = total + weights[tap_index] * moved * keep_mask[:, None]
    return total


def delta_rule(query, keyed, valued, rate, doc_ids):
    row_count, head_count, head_width = query.shape
    blocks = row_count // BLOCK
    float_type = query.dtype

    def to_blocks(array):
        return array.reshape(blocks, BLOCK, head_count, head_width).transpose(0, 2, 1, 3)

    query_blk = to_blocks(query)
    key_blk = to_blocks(keyed)
    value_blk = to_blocks(valued)
    rate_blk = rate.reshape(blocks, BLOCK, head_count).transpose(0, 2, 1)
    doc_blk = doc_ids.reshape(blocks, BLOCK)
    prior_doc = jnp.concatenate([jnp.full((1,), -1, jnp.int32), doc_blk[:-1, -1]])
    carry_in = (doc_blk == prior_doc[:, None]).astype(float_type)
    same_doc = doc_blk[:, :, None] == doc_blk[:, None, :]
    positions = jnp.arange(BLOCK)
    strict = positions[:, None] > positions[None, :]
    inclusive = positions[:, None] >= positions[None, :]
    key_key = jnp.einsum("nhtd,nhsd->nhts", key_blk, key_blk, precision=lax.Precision.HIGHEST)
    mixing = key_key * rate_blk[..., None] * (same_doc & strict)[:, None].astype(float_type)
    system = mixing + jnp.eye(BLOCK, dtype=float_type)
    scaled_values = value_blk * rate_blk[..., None]
    scaled_keys = key_blk * (rate_blk * carry_in[:, None, :])[..., None]
    solved_values = jax.scipy.linalg.solve_triangular(
        system, scaled_values, lower=True, unit_diagonal=True
    )
    solved_keys = jax.scipy.linalg.solve_triangular(
        system, scaled_keys, lower=True, unit_diagonal=True
    )
    scores = jnp.einsum("nhtd,nhsd->nhts", query_blk, key_blk, precision=lax.Precision.HIGHEST)
    scores = scores * (same_doc & inclusive)[:, None].astype(float_type)
    last_same = (doc_blk == doc_blk[:, -1:]).astype(float_type)
    carry_end = carry_in[:, -1]

    def advance(memory, inputs):
        solved_v, solved_k, score_n, query_n, key_n, carry_n, last_n, end_n = inputs
        update = solved_v - jnp.einsum(
            "htk,hvk->htv", solved_k, memory, precision=lax.Precision.HIGHEST
        )
        output = carry_n[None, :, None] * jnp.einsum(
            "hvk,htk->htv", memory, query_n, precision=lax.Precision.HIGHEST
        )
        output = output + jnp.einsum(
            "hts,hsv->htv", score_n, update, precision=lax.Precision.HIGHEST
        )
        memory = end_n * memory + jnp.einsum(
            "htv,htk->hvk", update * last_n[None, :, None], key_n, precision=lax.Precision.HIGHEST
        )
        return (memory, output)

    initial = jnp.zeros((head_count, head_width, head_width), float_type)
    _, outputs = lax.scan(
        advance,
        initial,
        (solved_values, solved_keys, scores, query_blk, key_blk, carry_in, last_same, carry_end),
    )
    return outputs.transpose(0, 2, 1, 3).reshape(row_count, head_count, head_width)


def mixer(
    query_raw,
    key_raw,
    value_raw,
    gating_raw,
    beta_raw,
    conv_q,
    conv_k,
    conv_v,
    gain_head,
    doc_ids,
    live,
):
    head_width = gain_head.shape[0]
    row_count = query_raw.shape[0]
    query_unit = jax.nn.silu(short_conv(query_raw, conv_q, doc_ids)).reshape(
        row_count, -1, head_width
    )
    query_unit = query_unit * lax.rsqrt(
        jnp.sum(query_unit * query_unit, axis=-1, keepdims=True) + 1e-06
    )
    key_unit = jax.nn.silu(short_conv(key_raw, conv_k, doc_ids)).reshape(row_count, -1, head_width)
    key_unit = key_unit * lax.rsqrt(jnp.sum(key_unit * key_unit, axis=-1, keepdims=True) + 1e-06)
    value_rows = jax.nn.silu(short_conv(value_raw, conv_v, doc_ids)).reshape(
        row_count, -1, head_width
    )
    beta_rate = jax.nn.sigmoid(beta_raw) * live[:, None]
    mixed = delta_rule(query_unit, key_unit, value_rows, beta_rate, doc_ids)
    norm_scale = lax.rsqrt(jnp.mean(mixed * mixed, axis=-1, keepdims=True) + 1e-05)
    gated = (
        mixed * norm_scale * gain_head * jax.nn.silu(gating_raw.reshape(row_count, -1, head_width))
    )
    gated = gated * live[:, None, None]
    return gated.reshape(row_count, -1)


def matmul(left, right):
    return jnp.dot(left, right, preferred_element_type=jnp.float32)


def matmul_nt(left, right):
    return lax.dot_general(
        left, right, (((1,), (1,)), ((), ())), preferred_element_type=jnp.float32
    )


def matmul_tn(left, right):
    return lax.dot_general(
        left, right, (((0,), (0,)), ((), ())), preferred_element_type=jnp.float32
    )


def gather_rows(rows):
    return lax.all_gather(rows, "tensor", axis=0, tiled=True)


def scatter_rows(partial_rows):
    return lax.psum_scatter(partial_rows, "tensor", scatter_dimension=0, tiled=True)


def fetch_mixer(first_gain, w_query, w_key, w_value, w_gating, w_beta, w_project):
    return (
        lax.all_gather(first_gain, "fsdp", axis=0, tiled=True),
        lax.all_gather(w_query, "fsdp", axis=0, tiled=True),
        lax.all_gather(w_key, "fsdp", axis=0, tiled=True),
        lax.all_gather(w_value, "fsdp", axis=0, tiled=True),
        lax.all_gather(w_gating, "fsdp", axis=0, tiled=True),
        lax.all_gather(w_beta, "fsdp", axis=0, tiled=True),
        lax.all_gather(w_project, "fsdp", axis=1, tiled=True),
    )


def fetch_ffn(second_gain, w_gate, w_up, w_down):
    return (
        lax.all_gather(second_gain, "fsdp", axis=0, tiled=True),
        lax.all_gather(w_gate, "fsdp", axis=0, tiled=True),
        lax.all_gather(w_up, "fsdp", axis=0, tiled=True),
        lax.all_gather(w_down, "fsdp", axis=1, tiled=True),
    )


def body(
    layer_input,
    first_gain,
    w_query,
    w_key,
    w_value,
    w_gating,
    w_beta,
    conv_query,
    conv_key,
    conv_value,
    head_gain,
    w_project,
    second_gain,
    w_gate,
    w_up,
    w_down,
    doc_starts,
    seq_lengths,
    output_grad,
):
    input_float = layer_input.astype(jnp.float32)
    seq_rows = layer_input.shape[0] * lax.axis_size("tensor")
    positions = jnp.arange(seq_rows, dtype=jnp.int32)
    doc_ids = jnp.sum((doc_starts[0][None, :] <= positions[:, None]).astype(jnp.int32), axis=1)
    live = (positions < seq_lengths[0]).astype(jnp.float32)
    conv_q = conv_query.astype(jnp.float32)
    conv_k = conv_key.astype(jnp.float32)
    conv_v = conv_value.astype(jnp.float32)
    gain_head = head_gain.astype(jnp.float32)
    gain_one, query_full, key_full, value_full, gating_full, beta_full, project_full = fetch_mixer(
        first_gain, w_query, w_key, w_value, w_gating, w_beta, w_project
    )
    scale_one = rms_scale(input_float)
    normed1 = (input_float * scale_one * gain_one.astype(jnp.float32)).astype(jnp.bfloat16)
    rows_one = gather_rows(normed1)
    query_raw = matmul(rows_one, query_full)
    key_raw = matmul(rows_one, key_full)
    value_raw = matmul(rows_one, value_full)
    gating_raw = matmul(rows_one, gating_full)
    beta_raw = matmul(rows_one, beta_full)

    def mixer_local(
        query_in, key_in, value_in, gating_in, beta_in, conv_qin, conv_kin, conv_vin, gain_in
    ):
        return mixer(
            query_in,
            key_in,
            value_in,
            gating_in,
            beta_in,
            conv_qin,
            conv_kin,
            conv_vin,
            gain_in,
            doc_ids,
            live,
        )

    mixer_inputs = (
        query_raw,
        key_raw,
        value_raw,
        gating_raw,
        beta_raw,
        conv_q,
        conv_k,
        conv_v,
        gain_head,
    )
    gated_float, pullback = jax.vjp(mixer_local, *mixer_inputs)
    gated = gated_float.astype(jnp.bfloat16)
    attn_out = scatter_rows(matmul(gated, project_full))
    resid = input_float + attn_out
    gain_two, gate_full, up_full, down_full = fetch_ffn(second_gain, w_gate, w_up, w_down)
    scale_two = rms_scale(resid)
    normed2 = (resid * scale_two * gain_two.astype(jnp.float32)).astype(jnp.bfloat16)
    rows_two = gather_rows(normed2)
    gate_val = matmul(rows_two, gate_full)
    up_val = matmul(rows_two, up_full)
    gate_sig = jax.nn.sigmoid(gate_val)
    silu_gate = gate_val * gate_sig
    hidden = (silu_gate * up_val).astype(jnp.bfloat16)
    ffn_out = scatter_rows(matmul(hidden, down_full))
    result = (resid + ffn_out).astype(jnp.bfloat16)
    gain_two, gate_full, up_full, down_full = fetch_ffn(second_gain, w_gate, w_up, w_down)
    grad_rows = gather_rows(output_grad)
    d_hidden = matmul_nt(grad_rows, down_full)
    grad_down = matmul_tn(hidden, grad_rows)
    d_gate = (d_hidden * up_val * gate_sig * (1.0 + gate_val * (1.0 - gate_sig))).astype(
        jnp.bfloat16
    )
    d_up = (d_hidden * silu_gate).astype(jnp.bfloat16)
    grad_gate = matmul_tn(rows_two, d_gate)
    grad_up = matmul_tn(rows_two, d_up)
    d_normed2 = scatter_rows(matmul_nt(d_gate, gate_full) + matmul_nt(d_up, up_full))
    grad_second = jnp.sum(d_normed2 * resid * scale_two, axis=0)
    d_resid = output_grad.astype(jnp.float32) + rms_back(
        resid, scale_two, gain_two.astype(jnp.float32), d_normed2
    )
    gain_one, query_full, key_full, value_full, gating_full, beta_full, project_full = fetch_mixer(
        first_gain, w_query, w_key, w_value, w_gating, w_beta, w_project
    )
    d_attn = gather_rows(d_resid.astype(jnp.bfloat16))
    d_gated = matmul_nt(d_attn, project_full)
    grad_project = matmul_tn(gated, d_attn)
    cotangents = pullback(d_gated)
    d_query = cotangents[0].astype(jnp.bfloat16)
    d_key = cotangents[1].astype(jnp.bfloat16)
    d_value = cotangents[2].astype(jnp.bfloat16)
    d_gating = cotangents[3].astype(jnp.bfloat16)
    d_beta = cotangents[4].astype(jnp.bfloat16)
    grad_query = matmul_tn(rows_one, d_query)
    grad_key = matmul_tn(rows_one, d_key)
    grad_value = matmul_tn(rows_one, d_value)
    grad_gating = matmul_tn(rows_one, d_gating)
    grad_beta = matmul_tn(rows_one, d_beta)
    d_norm_one = (
        matmul_nt(d_query, query_full) + matmul_nt(d_key, key_full) + matmul_nt(d_value, value_full)
    )
    d_norm_one = d_norm_one + matmul_nt(d_gating, gating_full) + matmul_nt(d_beta, beta_full)
    d_normed1 = scatter_rows(d_norm_one)
    grad_first = jnp.sum(d_normed1 * input_float * scale_one, axis=0)
    input_grad = d_resid + rms_back(input_float, scale_one, gain_one.astype(jnp.float32), d_normed1)
    gain_totals = lax.psum((grad_first, grad_second, cotangents[8]), "tensor")
    conv_totals = lax.psum(
        (cotangents[5], cotangents[6], cotangents[7], gain_totals[2]), ("dp", "fsdp")
    )
    shards = (
        lax.psum_scatter(
            gain_totals[0].astype(jnp.bfloat16), ("dp", "fsdp"), scatter_dimension=0, tiled=True
        ).astype(jnp.float32),
        lax.psum_scatter(
            grad_query.astype(jnp.bfloat16), ("dp", "fsdp"), scatter_dimension=0, tiled=True
        ).astype(jnp.float32),
        lax.psum_scatter(
            grad_key.astype(jnp.bfloat16), ("dp", "fsdp"), scatter_dimension=0, tiled=True
        ).astype(jnp.float32),
        lax.psum_scatter(
            grad_value.astype(jnp.bfloat16), ("dp", "fsdp"), scatter_dimension=0, tiled=True
        ).astype(jnp.float32),
        lax.psum_scatter(
            grad_gating.astype(jnp.bfloat16), ("dp", "fsdp"), scatter_dimension=0, tiled=True
        ).astype(jnp.float32),
        lax.psum_scatter(
            grad_beta.astype(jnp.bfloat16), ("dp", "fsdp"), scatter_dimension=0, tiled=True
        ).astype(jnp.float32),
        lax.psum_scatter(
            grad_project.astype(jnp.bfloat16), ("dp", "fsdp"), scatter_dimension=1, tiled=True
        ).astype(jnp.float32),
        lax.psum_scatter(
            gain_totals[1].astype(jnp.bfloat16), ("dp", "fsdp"), scatter_dimension=0, tiled=True
        ).astype(jnp.float32),
        lax.psum_scatter(
            grad_gate.astype(jnp.bfloat16), ("dp", "fsdp"), scatter_dimension=0, tiled=True
        ).astype(jnp.float32),
        lax.psum_scatter(
            grad_up.astype(jnp.bfloat16), ("dp", "fsdp"), scatter_dimension=0, tiled=True
        ).astype(jnp.float32),
        lax.psum_scatter(
            grad_down.astype(jnp.bfloat16), ("dp", "fsdp"), scatter_dimension=1, tiled=True
        ).astype(jnp.float32),
    )
    return (
        result,
        input_grad,
        shards[0],
        shards[1],
        shards[2],
        shards[3],
        shards[4],
        shards[5],
        conv_totals[0],
        conv_totals[1],
        conv_totals[2],
        conv_totals[3],
        shards[6],
        shards[7],
        shards[8],
        shards[9],
        shards[10],
    )


def solution(mesh):
    placed = (
        P(("dp", "fsdp", "tensor"), None),
        P("fsdp"),
        P("fsdp", "tensor"),
        P("fsdp", "tensor"),
        P("fsdp", "tensor"),
        P("fsdp", "tensor"),
        P("fsdp", "tensor"),
        P(None, "tensor"),
        P(None, "tensor"),
        P(None, "tensor"),
        P(),
        P("tensor", "fsdp"),
        P("fsdp"),
        P("fsdp", "tensor"),
        P("fsdp", "tensor"),
        P("tensor", "fsdp"),
        P(("dp", "fsdp"), None),
        P(("dp", "fsdp")),
        P(("dp", "fsdp", "tensor"), None),
    )
    return jax.shard_map(
        body,
        mesh=mesh,
        in_specs=placed,
        out_specs=(
            P(("dp", "fsdp", "tensor"), None),
            P(("dp", "fsdp", "tensor"), None),
            P(("dp", "fsdp")),
            P(("dp", "fsdp"), "tensor"),
            P(("dp", "fsdp"), "tensor"),
            P(("dp", "fsdp"), "tensor"),
            P(("dp", "fsdp"), "tensor"),
            P(("dp", "fsdp"), "tensor"),
            P(None, "tensor"),
            P(None, "tensor"),
            P(None, "tensor"),
            P(),
            P("tensor", ("dp", "fsdp")),
            P(("dp", "fsdp")),
            P(("dp", "fsdp"), "tensor"),
            P(("dp", "fsdp"), "tensor"),
            P("tensor", ("dp", "fsdp")),
        ),
        check_vma=False,
    )
```

profile of v0, /device:TPU:0, one launch (start us, length us, event | category | flops | bytes accessed | tf_op | source)
XLA Modules:
  0.0 1605.7 jit_solution(16888827830021161958)
XLA Ops:
  26.4 19.2 %all-gather.19.cloned.1.call-done = bf16[2048,512]{1,0:T(8,128)(2,1)} async-done(((bf16[1024,512]{1,0:T(8,128)(2,1)}), bf16[2048,512]{1,0:T(8,128)(2,1)}) %all-gather.19.cloned.1.call-update) | async-done | bytes 2097168 | tf_op jit(solution)/shard_map/all_gather | solution.py:155
  45.6 48.2 %all-gather.13.cloned.1.call-done = bf16[512,2048]{1,0:T(8,128)(2,1)} async-done(((bf16[128,2048]{1,0:T(8,128)(2,1)}), bf16[512,2048]{1,0:T(8,128)(2,1)}) %all-gather.13.cloned.1.call-update) | async-done | bytes 2097168 | tf_op jit(solution)/shard_map/all_gather | solution.py:145
  98.4 28.8 %all-gather.17.cloned.1.call-done = bf16[2048,512]{1,0:T(8,128)(2,1)} async-done(((bf16[1024,512]{1,0:T(8,128)(2,1)}), bf16[2048,512]{1,0:T(8,128)(2,1)}) %all-gather.17.cloned.1.call-update) | async-done | bytes 2097168 | tf_op jit(solution)/shard_map/all_gather | solution.py:157
  136.1 25.6 %all-gather.15.cloned.1.call-done = bf16[2048,512]{1,0:T(8,128)(2,1)} async-done(((bf16[1024,512]{1,0:T(8,128)(2,1)}), bf16[2048,512]{1,0:T(8,128)(2,1)}) %all-gather.15.cloned.1.call-update) | async-done | bytes 2097168 | tf_op jit(solution)/shard_map/all_gather | solution.py:156
  182.0 158.2 %custom-call.12 = f32[8,4,1,64,64]{3,4,2,1,0:T(8,128)S(1)} custom-call(f32[8,4,1,64,64]{4,3,2,1,0:T(8,128)} %add_bitcast_fusion), custom_call_target="InvertDiagBlocksLowerTriangular" | custom-call | tf_op jit(solution)/shard_map/jvp(jit(_solve_triangular))/vmap(vmap())/triangular_solve | solution.py:56
  356.3 70.5 %while.48 = (s32[]{:T(128)}, f32[4,128,128]{2,1,0:T(8,128)S(1)}, f32[8,4,64,128]{3,2,1,0:T(8,128)}, f32[8,4,128,128]{3,2,1,0:T(8,128)}, f32[8,1,64,1]{2,3,1,0:T(...) while((s32[]{:T(128)}, f32[4,128,128]{2,1,0:T(8,128)S(1)}, ...), condition=%wide.region_5.7_spmd.clone, body=%wide.region_4.6_spmd.clone.sunk | while | flops 176717824 | bytes 3283676 | solution.py:84
  447.0 71.4 %reduce-scatter.16.cloned.1.call-done = f32[128,2048]{1,0:T(8,128)} async-done(((f32[512,2048]{1,0:T(8,128)}), f32[128,2048]{1,0:T(8,128)}) %reduce-scatter.16.cloned.1.call-update) | async-done | bytes 1048592 | tf_op jit(solution)/shard_map/reduce_scatter | solution.py:149
  522.9 72.1 %all-gather.27.cloned.1.call-done = bf16[2048,1408]{1,0:T(8,128)(2,1)} async-done(((bf16[1024,1408]{1,0:T(8,128)(2,1)}), bf16[2048,1408]{1,0:T(8,128)(2,1)}) %all-gather.27.cloned.1.call-update) | async-done | bytes 5767184 | tf_op jit(solution)/shard_map/all_gather | solution.py:167
  595.0 48.2 %all-gather.25.cloned.1.call-done = bf16[512,2048]{1,0:T(8,128)(2,1)} async-done(((bf16[128,2048]{1,0:T(8,128)(2,1)}), bf16[512,2048]{1,0:T(8,128)(2,1)}) %all-gather.25.cloned.1.call-update) | async-done | bytes 2097168 | tf_op jit(solution)/shard_map/all_gather | solution.py:145
  643.2 8.2 fusion.186
  651.4 66.4 %all-gather.29.cloned.1.call-done = bf16[2048,1408]{1,0:T(8,128)(2,1)} async-done(((bf16[1024,1408]{1,0:T(8,128)(2,1)}), bf16[2048,1408]{1,0:T(8,128)(2,1)}) %all-gather.29.cloned.1.call-update) | async-done | bytes 5767184 | tf_op jit(solution)/shard_map/all_gather | solution.py:168
  717.9 8.3 fusion.187
  726.2 39.3 %all-gather.33.cloned.1.call-done = bf16[512,2048]{1,0:T(8,128)(2,1)} async-done(((bf16[128,2048]{1,0:T(8,128)(2,1)}), bf16[512,2048]{1,0:T(8,128)(2,1)}) %all-gather.33.cloned.1.call-update) | async-done | bytes 2097168 | tf_op jit(solution)/shard_map/all_gather | solution.py:145
  765.5 74.7 %all-gather.31.cloned.1.call-done = bf16[1408,2048]{1,0:T(8,128)(2,1)} async-done(((bf16[1408,1024]{1,0:T(8,128)(2,1)}), bf16[1408,2048]{1,0:T(8,128)(2,1)}) %all-gather.31.cloned.1.call-update) | async-done | bytes 5767184 | tf_op jit(solution)/shard_map/all_gather | solution.py:169
  840.2 10.4 multiply_convert_fusion
  862.3 76.9 %reduce-scatter.20.cloned.1.call-done = f32[128,2048]{1,0:T(8,128)} async-done(((f32[512,2048]{1,0:T(8,128)}), f32[128,2048]{1,0:T(8,128)}) %reduce-scatter.20.cloned.1.call-update) | async-done | bytes 1048592 | tf_op jit(solution)/shard_map/reduce_scatter | solution.py:149
  942.3 7.9 convolution_convert_fusion.2
  950.3 8.1 convolution_convert_fusion.1
  963.3 7.7 convolution_convert_fusion
  971.1 17.5 %all-gather.35.cloned.1.call-done = bf16[512,2048]{1,0:T(8,128)(2,1)} async-done(((bf16[128,2048]{1,0:T(8,128)(2,1)}), bf16[512,2048]{1,0:T(8,128)(2,1)}) %all-gather.35.cloned.1.call-update) | async-done | bytes 2097168 | tf_op jit(solution)/shard_map/all_gather | solution.py:145
  1007.6 126.0 %while.49 = (s32[]{:T(128)}, f32[4,128,128]{2,1,0:T(8,128)S(1)}, f32[8,4,64,128]{3,2,1,0:T(8,128)}, f32[8,4,64,128]{3,2,1,0:T(8,128)}, f32[8,4,64,64]{3,2,1,0:T(...) while((s32[]{:T(128)}, f32[4,128,128]{2,1,0:T(8,128)S(1)}, ...), condition=%wide.region_14.16_spmd.clone, body=%wide.region_13.15_spmd.clone.sunk | while | flops 352911360 | bytes 4731118 | solution.py:84
  1218.3 7.5 fusion.188
  1236.4 21.0 %reduce-scatter.24.cloned.1.call-done = bf16[256,512]{1,0:T(8,128)(2,1)} async-done(((bf16[2048,512]{1,0:T(8,128)(2,1)}), bf16[256,512]{1,0:T(8,128)(2,1)}) %reduce-scatter.24.cloned.1.call-update) | async-done | bytes 262160 | tf_op jit(solution)/shard_map/reduce_scatter | solution.py:305
  1259.2 43.0 %reduce-scatter.26.cloned.1.call-done = bf16[256,512]{1,0:T(8,128)(2,1)} async-done(((bf16[2048,512]{1,0:T(8,128)(2,1)}), bf16[256,512]{1,0:T(8,128)(2,1)}) %reduce-scatter.26.cloned.1.call-update) | async-done | bytes 262160 | tf_op jit(solution)/shard_map/reduce_scatter | solution.py:308
  1304.0 42.7 %reduce-scatter.28.cloned.1.call-done = bf16[256,512]{1,0:T(8,128)(2,1)} async-done(((bf16[2048,512]{1,0:T(8,128)(2,1)}), bf16[256,512]{1,0:T(8,128)(2,1)}) %reduce-scatter.28.cloned.1.call-update) | async-done | bytes 262160 | tf_op jit(solution)/shard_map/reduce_scatter | solution.py:311
  1348.5 43.1 %reduce-scatter.30.cloned.1.call-done = bf16[256,512]{1,0:T(8,128)(2,1)} async-done(((bf16[2048,512]{1,0:T(8,128)(2,1)}), bf16[256,512]{1,0:T(8,128)(2,1)}) %reduce-scatter.30.cloned.1.call-update) | async-done | bytes 262160 | tf_op jit(solution)/shard_map/reduce_scatter | solution.py:314
  1393.4 42.8 %reduce-scatter.32.cloned.1.call-done = bf16[512,256]{1,0:T(8,128)(2,1)} async-done(((bf16[512,2048]{1,0:T(8,128)(2,1)}), bf16[512,256]{1,0:T(8,128)(2,1)}) %reduce-scatter.32.cloned.1.call-update) | async-done | bytes 262160 | tf_op jit(solution)/shard_map/reduce_scatter | solution.py:320
  1438.0 77.3 %reduce-scatter.22.cloned.1.call-done = f32[128,2048]{1,0:T(8,128)} async-done(((f32[512,2048]{1,0:T(8,128)}), f32[128,2048]{1,0:T(8,128)}) %reduce-scatter.22.cloned.1.call-update) | async-done | bytes 1048592 | tf_op jit(solution)/shard_map/reduce_scatter | solution.py:149
  1516.7 18.8 %all-reduce.36 = (bf16[2048]{0:T(1024)(128)(2,1)S(1)}, f32[128]{0:T(128)S(1)}, bf16[2048]{0:T(1024)(128)(2,1)S(1)}) all-reduce(f32[2048]{0:T(1024)S(1)} %get-tuple-element.717, f32[128]{0:T(128)S(1)} %copy-done.107, f32[2048]{0:T(1024)S(1)} %get-tuple-element.701), channel_id=1, replica_groups=mesh['dp'=4,'fsdp'=2,'tensor'=4] {'tensor'}, use_global_device_ids=true, to_apply=%region_23.26 | all-reduce | flops 4224 | bytes 25600 | tf_op jit(solution)/shard_map/psum | solution.py:297
  1535.6 14.6 all-reduce.37
  1550.2 24.6 %all-reduce.35 = (f32[4,512]{1,0:T(4,128)}, f32[4,512]{1,0:T(4,128)}, f32[4,512]{1,0:T(4,128)}, f32[128]{0:T(128)}) all-reduce(f32[4,512]{1,0:T(4,128)S(1)} %pad_add_fusion.2, f32[4,512]{1,0:T(4,128)S(1)} %pad_add_fusion.1, f32[4,512]{1,0:T(4,128)S(1)} %pad_add_fusion, ...), channel_id=1, replica_groups=mesh['dp'=4,'fsdp'=2,'tensor'=4] {'dp','fsdp'}, use_global_device_ids=true, to_apply=%region_34.37 | all-reduce | flops 6272 | bytes 50176 | tf_op jit(solution)/shard_map/psum | solution.py:298
  1576.1 19.3 %reduce-scatter.18.cloned.1.call-done = f32[128,2048]{1,0:T(8,128)} async-done(((f32[512,2048]{1,0:T(8,128)}), f32[128,2048]{1,0:T(8,128)}) %reduce-scatter.18.cloned.1.call-update) | async-done | bytes 1048592 | tf_op jit(solution)/shard_map/reduce_scatter | solution.py:149
  (596 shorter events, 435.6 us)
Async XLA Ops:
  7.2 38.4 %all-gather.19.cloned.1.call-start = ((), (), s32[]{:S(2)}) async-start(), calls=%async_computation.16 | async-start | bytes 3145728 | tf_op jit(solution)/shard_map/all_gather | solution.py:155
  7.9 85.8 %all-gather.13.cloned.1.call-start = ((), (), s32[]{:S(2)}) async-start(), calls=%async_computation.13 | async-start | bytes 2621440 | tf_op jit(solution)/shard_map/all_gather | solution.py:145
  16.8 110.4 %all-gather.17.cloned.1.call-start = ((), (), s32[]{:S(2)}) async-start(), calls=%async_computation.15 | async-start | bytes 3145728 | tf_op jit(solution)/shard_map/all_gather | solution.py:157
  17.5 144.2 %all-gather.15.cloned.1.call-start = ((), (), s32[]{:S(2)}) async-start(), calls=%async_computation.14 | async-start | bytes 3145728 | tf_op jit(solution)/shard_map/all_gather | solution.py:156
  18.1 412.2 %all-gather.21.cloned.1.call-start = ((), (), s32[]{:S(2)}) async-start(), calls=%async_computation.17 | async-start | bytes 3145728 | tf_op jit(solution)/shard_map/all_gather | solution.py:158
  18.7 417.6 %all-gather.23.cloned.1.call-start = ((), (), s32[]{:S(2)}) async-start(), calls=%async_computation.18 | async-start | bytes 3145728 | tf_op jit(solution)/shard_map/all_gather | solution.py:160
  19.3 499.0 %reduce-scatter.16.cloned.1.call-start = ((), (), s32[]{:S(2)}) async-start(), calls=%async_computation.19 | async-start | bytes 5242880 | tf_op jit(solution)/shard_map/reduce_scatter | solution.py:149
  20.7 410.2 %copy-start.69 = (f32[512]{0:T(512)}, f32[512]{0:T(512)S(1)}, u32[]{:S(2)}) copy-start(f32[512]{0:T(512)S(1)} %fusion.165) | copy-start | bytes 6148
  20.8 410.1 %copy-start.105 = (f32[512]{0:T(512)}, f32[512]{0:T(512)S(1)}, u32[]{:S(2)}) copy-start(f32[512]{0:T(512)S(1)} %broadcast_bitcast_fusion) | copy-start | bytes 6148
  26.4 323.8 %copy-start.42 = (f32[8,64,64]{2,1,0:T(8,128)}, f32[8,64,64]{2,1,0:T(8,128)S(1)}, u32[]{:S(2)}) copy-start(f32[8,64,64]{2,1,0:T(8,128)S(1)} %get-tuple-element.848) | copy-start | bytes 393220
  441.4 153.6 %all-gather.27.cloned.1.call-start = ((), (), s32[]{:S(2)}) async-start(), calls=%async_computation.21 | async-start | bytes 8650752 | tf_op jit(solution)/shard_map/all_gather | solution.py:167
  442.1 201.1 %all-gather.25.cloned.1.call-start = ((), (), s32[]{:S(2)}) async-start(), calls=%async_computation.20 | async-start | bytes 2621440 | tf_op jit(solution)/shard_map/all_gather | solution.py:145
  519.9 420.9 %copy-start.96 = (f32[128]{0:T(128)}, f32[128]{0:T(128)S(1)}, u32[]{:S(2)}) copy-start(f32[128]{0:T(128)S(1)} %add_rsqrt_fusion.2) | copy-start | bytes 1540
  520.9 196.9 %all-gather.29.cloned.1.call-start = ((), (), s32[]{:S(2)}) async-start(), calls=%async_computation.22 | async-start | bytes 8650752 | tf_op jit(solution)/shard_map/all_gather | solution.py:168
  521.5 244.0 %all-gather.33.cloned.1.call-start = ((), (), s32[]{:S(2)}) async-start(), calls=%async_computation.25 | async-start | bytes 2621440 | tf_op jit(solution)/shard_map/all_gather | solution.py:145
  522.2 317.9 %all-gather.31.cloned.1.call-start = ((), (), s32[]{:S(2)}) async-start(), calls=%async_computation.23 | async-start | bytes 8650752 | tf_op jit(solution)/shard_map/all_gather | solution.py:169
  522.8 416.4 %reduce-scatter.20.cloned.1.call-start = ((), (), s32[]{:S(2)}) async-start(), calls=%async_computation.26 | async-start | bytes 5242880 | tf_op jit(solution)/shard_map/reduce_scatter | solution.py:149
  862.3 126.4 %all-gather.35.cloned.1.call-start = ((), (), s32[]{:S(2)}) async-start(), calls=%async_computation.27 | async-start | bytes 2621440 | tf_op jit(solution)/shard_map/all_gather | solution.py:145
  942.1 285.7 %reduce-scatter.34.cloned.1.call-start = ((), (), s32[]{:S(2)}) async-start(), calls=%async_computation.34 | async-start | bytes 6488064 | tf_op jit(solution)/shard_map/reduce_scatter | solution.py:326
  950.2 279.9 %reduce-scatter.36.cloned.1.call-start = ((), (), s32[]{:S(2)}) async-start(), calls=%async_computation.35 | async-start | bytes 6488064 | tf_op jit(solution)/shard_map/reduce_scatter | solution.py:329
  958.4 274.0 %reduce-scatter.38.cloned.1.call-start = ((), (), s32[]{:S(2)}) async-start(), calls=%async_computation.36 | async-start | bytes 6488064 | tf_op jit(solution)/shard_map/reduce_scatter | solution.py:332
  971.1 263.7 %reduce-scatter.40.cloned.1.call-start = ((), (), s32[]{:S(2)}) async-start(), calls=%async_computation.37 | async-start | bytes 589824
  1164.3 93.1 %reduce-scatter.24.cloned.1.call-start = ((), (), s32[]{:S(2)}) async-start(), calls=%async_computation.29 | async-start | bytes 2359296 | tf_op jit(solution)/shard_map/reduce_scatter | solution.py:305
  1180.8 121.4 %reduce-scatter.26.cloned.1.call-start = ((), (), s32[]{:S(2)}) async-start(), calls=%async_computation.30 | async-start | bytes 2359296 | tf_op jit(solution)/shard_map/reduce_scatter | solution.py:308
  1187.4 159.3 %reduce-scatter.28.cloned.1.call-start = ((), (), s32[]{:S(2)}) async-start(), calls=%async_computation.31 | async-start | bytes 2359296 | tf_op jit(solution)/shard_map/reduce_scatter | solution.py:311
  1194.3 197.3 %reduce-scatter.30.cloned.1.call-start = ((), (), s32[]{:S(2)}) async-start(), calls=%async_computation.32 | async-start | bytes 2359296 | tf_op jit(solution)/shard_map/reduce_scatter | solution.py:314
  1199.6 236.6 %reduce-scatter.32.cloned.1.call-start = ((), (), s32[]{:S(2)}) async-start(), calls=%async_computation.33 | async-start | bytes 2359296 | tf_op jit(solution)/shard_map/reduce_scatter | solution.py:320
  1204.8 310.4 %reduce-scatter.22.cloned.1.call-start = ((), (), s32[]{:S(2)}) async-start(), calls=%async_computation.28 | async-start | bytes 5242880 | tf_op jit(solution)/shard_map/reduce_scatter | solution.py:149
  1217.0 378.5 %reduce-scatter.18.cloned.1.call-start = ((), (), s32[]{:S(2)}) async-start(), calls=%async_computation.24 | async-start | bytes 5242880 | tf_op jit(solution)/shard_map/reduce_scatter | solution.py:149
  1304.0 291.5 %copy-start.9 = (f32[128,2048]{1,0:T(8,128)S(1)}, f32[128,2048]{1,0:T(8,128)}, u32[]{:S(2)}) copy-start(f32[128,2048]{1,0:T(8,128)} %reduce-scatter.20.cloned.1.call-done) | copy-start | bytes 3145732
  1304.0 291.5 %copy-start.24 = (bf16[128,2048]{1,0:T(8,128)(2,1)S(1)}, bf16[128,2048]{1,0:T(8,128)(2,1)}, u32[]{:S(2)}) copy-start(bf16[128,2048]{1,0:T(8,128)(2,1)} %param.47) | copy-start | bytes 1572868
  1304.0 291.5 %copy-start.97 = (f32[128]{0:T(128)S(1)}, f32[128]{0:T(128)}, u32[]{:S(2)}) copy-start(f32[128]{0:T(128)} %copy-done.96) | copy-start | bytes 1540
  (110 other events, 3390.7 us)
Sparse Core Ops, SparseCore 0:
  9.6 35.9 all-gather.18
  47.7 45.9 all-gather.12
  95.3 31.8 all-gather.16
  128.6 33.1 all-gather.14
  163.1 33.1 all-gather.20
  197.7 33.2 all-gather.22
  441.5 76.8 reduce-scatter.15
  520.0 74.9 all-gather.26
  597.2 45.9 all-gather.24
  644.6 73.1 all-gather.28
  719.5 45.9 all-gather.32
  767.0 73.1 all-gather.30
  862.4 76.7 reduce-scatter.19
  942.2 46.4 all-gather.34
  992.0 57.7 reduce-scatter.33
  1053.4 59.0 reduce-scatter.35
  1115.8 59.0 reduce-scatter.37
  1178.7 34.0 reduce-scatter.39
  1216.1 41.2 reduce-scatter.23
  1260.9 41.2 reduce-scatter.25
  1305.5 41.2 reduce-scatter.27
  1350.4 41.2 reduce-scatter.29
  1394.9 41.2 reduce-scatter.31
  1438.4 76.7 reduce-scatter.21
  1517.5 77.8 reduce-scatter.17
where the time goes:
time: 1620 us; the launch traced here: 1610 us
  waiting for transfers between devices  883 us (55%)
  matrix products  329 us (20%)
  other arithmetic  228 us (14%)
  local copies, waits for them, and re-layouts  73.6 us (5%)
  blocking collectives  72.9 us (5%)
  between operations  17.5 us (1%)
    reduce_scatter x4, waiting for transfers between devices, scatter_rows(): lax.psum_scatter(partial_rows, 'tensor', scatter_dimension=0, tiled=True)  245 us
    another operation x5, other arithmetic, delta_rule(): jax.scipy.linalg.solve_triangular(system, scaled_values, lower=True, unit...  160 us
    all_gather x4, waiting for transfers between devices, gather_rows(): return lax.all_gather(rows, 'tensor', axis=0, tiled=True)  153 us
    all_gather x1, waiting for transfers between devices, fetch_ffn(): lax.all_gather(w_down, 'fsdp', axis=1, tiled=True)  74.7 us
    all_gather x1, waiting for transfers between devices, fetch_ffn(): lax.all_gather(w_gate, 'fsdp', axis=0, tiled=True)  72.1 us
    all_gather x1, waiting for transfers between devices, fetch_ffn(): lax.all_gather(w_up, 'fsdp', axis=0, tiled=True)  66.4 us
    dot_general x24, matrix products, advance(): jnp.einsum('hvk,htk->htv', memory, query_n, precision=lax.Precision.HIGHEST)  52.5 us
    dot_general x9, matrix products, matmul(): return jnp.dot(left, right, preferred_element_type=jnp.float32)  47.9 us
  transfers between devices with their start and end apart: 25, of which 19 were waited for; matrix products, arithmetic and copies ran while one was open for 36% of the time, Pallas kernels for 0%

commit v1 on v0

--- a/solution.py
+++ b/solution.py
@@ -5,6 +5,18 @@
 
 KERNEL = 4
 BLOCK = 64
+
+
+def collect(shard, axis, dim):
+    ways, here = (lax.axis_size(axis), lax.axis_index(axis))
+    grown, reach = (shard, 1)
+    while reach < ways:
+        theirs = lax.ppermute(grown, axis, [(d, d ^ reach) for d in range(ways)])
+        mine_first = jnp.concatenate([grown, theirs], axis=dim)
+        theirs_first = jnp.concatenate([theirs, grown], axis=dim)
+        grown = jnp.where(here & reach == 0, mine_first, theirs_first)
+        reach = 2 * reach
+    return grown
 
 
 def rms_scale(values):
@@ -142,7 +154,7 @@
 
 
 def gather_rows(rows):
-    return lax.all_gather(rows, "tensor", axis=0, tiled=True)
+    return collect(rows, "tensor", 0)
 
 
 def scatter_rows(partial_rows):

time: 1620 us -> 1480 us (0.914)
  waiting for transfers between devices: 883 us -> 716 us
  starting transfers between devices: 1.44 us -> 17.9 us
    all_gather x4 -> x0, waiting for transfers between devices: 153 us -> none  [gather_rows(): return lax.all_gather(rows, 'tensor', axis=0, tiled=True)]
    ppermute x0 -> x8, waiting for transfers between devices: none -> 148 us  [collect(): theirs = lax.ppermute(grown, axis, [(d, d ^ reach) for d in range(ways)])]
    all_gather x1, waiting for transfers between devices: 72.1 us -> 20.5 us  [fetch_ffn(): lax.all_gather(w_gate, 'fsdp', axis=0, tiled=True)]
    all_gather x1, waiting for transfers between devices: 28.8 us -> 0.01 us  [fetch_mixer(): lax.all_gather(w_value, 'fsdp', axis=0, tiled=True)]
    reduce_scatter x4, waiting for transfers between devices: 245 us -> 225 us  [scatter_rows(): lax.psum_scatter(partial_rows, 'tensor', scatter_dimension=0, tiled=True)]
    all_gather x1, waiting for transfers between devices: 19.2 us -> 0.02 us  [fetch_mixer(): lax.all_gather(w_query, 'fsdp', axis=0, tiled=True)]
    ppermute x0 -> x8, starting transfers between devices: none -> 16.3 us  [collect(): theirs = lax.ppermute(grown, axis, [(d, d ^ reach) for d in range(ways)])]
  transfers between devices with their start and end apart: 25 -> 29, of which waited for: 19 -> 20; matrix products, arithmetic and copies ran while one was open for 36% -> 41% of each run, Pallas kernels for 0% -> 0%
where the time goes in v1:
time: 1480 us; the launch traced here: 1470 us
  waiting for transfers between devices  716 us (48%)
  matrix products  332 us (22%)
  other arithmetic  233 us (16%)
  local copies, waits for them, and re-layouts  75.7 us (5%)
  blocking collectives  72.4 us (5%)
  starting transfers between devices  17.9 us (1%)
  between operations  17.5 us (1%)
    reduce_scatter x4, waiting for transfers between devices, scatter_rows(): lax.psum_scatter(partial_rows, 'tensor', scatter_dimension=0, tiled=True)  225 us
    another operation x5, other arithmetic, delta_rule(): jax.scipy.linalg.solve_triangular(system, scaled_values, lower=True, unit...  160 us
    ppermute x8, waiting for transfers between devices, collect(): theirs = lax.ppermute(grown, axis, [(d, d ^ reach) for d in range(ways)])  148 us
    all_gather x1, waiting for transfers between devices, fetch_ffn(): lax.all_gather(w_down, 'fsdp', axis=1, tiled=True)  67.2 us
    all_gather x1, waiting for transfers between devices, fetch_ffn(): lax.all_gather(w_up, 'fsdp', axis=0, tiled=True)  54.8 us
    dot_general x24, matrix products, advance(): jnp.einsum('hvk,htk->htv', memory, query_n, precision=lax.Precision.HIGHEST)  52.5 us
    dot_general x9, matrix products, matmul(): return jnp.dot(left, right, preferred_element_type=jnp.float32)  46.9 us
    dot_general x24, matrix products, advance(): jnp.einsum('htk,hvk->htv', solved_k, memory, precision=lax.Precision.HIGH...  46.2 us
  transfers between devices with their start and end apart: 29, of which 20 were waited for; matrix products, arithmetic and copies ran while one was open for 41% of the time, Pallas kernels for 0%

profile of v1, /device:TPU:0, one launch (start us, length us, event | category | flops | bytes accessed | tf_op | source)
XLA Modules:
  0.0 1465.4 jit_solution(4742324829644785677)
XLA Ops:
  20.5 8.4 collective-permute-done
  36.9 39.0 %collective-permute-done.1 = bf16[256,2048]{1,0:T(8,128)(2,1)} collective-permute-done((bf16[256,2048]{1,0:T(8,128)(2,1)S(1)}, bf16[256,2048]{1,0:T(8,128)(2,1)}, u32[]{:S(2)}, u32[]{:S(2)}) %collective-permute-start.1) | collective-permute-done | bytes 1048608 | tf_op jit(solution)/shard_map/ppermute | solution.py:14
  97.0 18.1 %all-gather.9.cloned.1.call-done = bf16[2048,512]{1,0:T(8,128)(2,1)} async-done(((bf16[1024,512]{1,0:T(8,128)(2,1)}), bf16[2048,512]{1,0:T(8,128)(2,1)}) %all-gather.9.cloned.1.call-update) | async-done | bytes 2097168 | tf_op jit(solution)/shard_map/all_gather | solution.py:168
  132.4 158.4 %custom-call.12 = f32[8,4,1,64,64]{3,4,2,1,0:T(8,128)S(1)} custom-call(f32[8,4,1,64,64]{4,3,2,1,0:T(8,128)} %add_bitcast_fusion), custom_call_target="InvertDiagBlocksLowerTriangular" | custom-call | tf_op jit(solution)/shard_map/jvp(jit(_solve_triangular))/vmap(vmap())/triangular_solve | solution.py:68
  306.8 70.5 %while.48 = (s32[]{:T(128)}, f32[4,128,128]{2,1,0:T(8,128)S(1)}, f32[8,4,64,128]{3,2,1,0:T(8,128)}, f32[8,4,128,128]{3,2,1,0:T(8,128)}, f32[8,1,64,1]{2,3,1,0:T(...) while((s32[]{:T(128)}, f32[4,128,128]{2,1,0:T(8,128)S(1)}, ...), condition=%wide.region_5.7_spmd.clone, body=%wide.region_4.6_spmd.clone.sunk | while | flops 176717824 | bytes 3283676 | solution.py:96
  398.7 70.2 %reduce-scatter.16.cloned.1.call-done = f32[128,2048]{1,0:T(8,128)} async-done(((f32[512,2048]{1,0:T(8,128)}), f32[128,2048]{1,0:T(8,128)}) %reduce-scatter.16.cloned.1.call-update) | async-done | bytes 1048592 | tf_op jit(solution)/shard_map/reduce_scatter | solution.py:161
  472.2 12.2 collective-permute-done.2
  489.1 32.7 %collective-permute-done.4 = bf16[128,2048]{1,0:T(8,128)(2,1)S(1)} collective-permute-done((bf16[128,2048]{1,0:T(8,128)(2,1)S(1)}, bf16[128,2048]{1,0:T(8,128)(2,1)S(1)}, u32[]{:S(2)}, u32[]{:S(2)}) %collective-permute-start.4) | collective-permute-done | bytes 524320 | tf_op jit(solution)/shard_map/ppermute | solution.py:14
  525.0 20.5 %all-gather.19.cloned.1.call-done = bf16[2048,1408]{1,0:T(8,128)(2,1)} async-done(((bf16[1024,1408]{1,0:T(8,128)(2,1)}), bf16[2048,1408]{1,0:T(8,128)(2,1)}) %all-gather.19.cloned.1.call-update) | async-done | bytes 5767184 | tf_op jit(solution)/shard_map/all_gather | solution.py:179
  545.5 11.6 collective-permute-done.3
  557.1 9.8 fusion.179
  566.9 54.8 %all-gather.21.cloned.1.call-done = bf16[2048,1408]{1,0:T(8,128)(2,1)} async-done(((bf16[1024,1408]{1,0:T(8,128)(2,1)}), bf16[2048,1408]{1,0:T(8,128)(2,1)}) %all-gather.21.cloned.1.call-update) | async-done | bytes 5767184 | tf_op jit(solution)/shard_map/all_gather | solution.py:180
  621.6 8.9 fusion.178
  630.6 67.2 %all-gather.23.cloned.1.call-done = bf16[1408,2048]{1,0:T(8,128)(2,1)} async-done(((bf16[1408,1024]{1,0:T(8,128)(2,1)}), bf16[1408,2048]{1,0:T(8,128)(2,1)}) %all-gather.23.cloned.1.call-update) | async-done | bytes 5767184 | tf_op jit(solution)/shard_map/all_gather | solution.py:181
  697.8 11.0 multiply_convert_fusion
  720.8 8.7 convolution_convert_fusion.2
  729.6 8.7 convolution_convert_fusion.1
  738.7 58.8 %reduce-scatter.20.cloned.1.call-done = f32[128,2048]{1,0:T(8,128)} async-done(((f32[512,2048]{1,0:T(8,128)}), f32[128,2048]{1,0:T(8,128)}) %reduce-scatter.20.cloned.1.call-update) | async-done | bytes 1048592 | tf_op jit(solution)/shard_map/reduce_scatter | solution.py:161
  801.1 12.2 collective-permute-done.6
  822.4 8.5 convolution_convert_fusion
  830.9 31.7 %collective-permute-done.7 = bf16[256,2048]{1,0:T(8,128)(2,1)} collective-permute-done((bf16[256,2048]{1,0:T(8,128)(2,1)}, bf16[256,2048]{1,0:T(8,128)(2,1)}, u32[]{:S(2)}, u32[]{:S(2)}) %collective-permute-start.7) | collective-permute-done | bytes 1048608 | tf_op jit(solution)/shard_map/ppermute | solution.py:14
  882.4 125.5 %while.49 = (s32[]{:T(128)}, f32[4,128,128]{2,1,0:T(8,128)S(1)}, f32[8,4,64,128]{3,2,1,0:T(8,128)}, f32[8,4,64,128]{3,2,1,0:T(8,128)}, f32[8,4,64,64]{3,2,1,0:T(...) while((s32[]{:T(128)}, f32[4,128,128]{2,1,0:T(8,128)S(1)}, ...), condition=%wide.region_14.16_spmd.clone, body=%wide.region_13.15_spmd.clone.sunk | while | flops 352911360 | bytes 4731118 | solution.py:96
  1093.2 7.5 fusion.194
  1119.2 42.9 %reduce-scatter.26.cloned.1.call-done = bf16[256,512]{1,0:T(8,128)(2,1)} async-done(((bf16[2048,512]{1,0:T(8,128)(2,1)}), bf16[256,512]{1,0:T(8,128)(2,1)}) %reduce-scatter.26.cloned.1.call-update) | async-done | bytes 262160 | tf_op jit(solution)/shard_map/reduce_scatter | solution.py:320
  1164.0 42.5 %reduce-scatter.28.cloned.1.call-done = bf16[256,512]{1,0:T(8,128)(2,1)} async-done(((bf16[2048,512]{1,0:T(8,128)(2,1)}), bf16[256,512]{1,0:T(8,128)(2,1)}) %reduce-scatter.28.cloned.1.call-update) | async-done | bytes 262160 | tf_op jit(solution)/shard_map/reduce_scatter | solution.py:323
  1208.3 42.9 %reduce-scatter.30.cloned.1.call-done = bf16[256,512]{1,0:T(8,128)(2,1)} async-done(((bf16[2048,512]{1,0:T(8,128)(2,1)}), bf16[256,512]{1,0:T(8,128)(2,1)}) %reduce-scatter.30.cloned.1.call-update) | async-done | bytes 262160 | tf_op jit(solution)/shard_map/reduce_scatter | solution.py:326
  1253.1 42.8 %reduce-scatter.32.cloned.1.call-done = bf16[512,256]{1,0:T(8,128)(2,1)} async-done(((bf16[512,2048]{1,0:T(8,128)(2,1)}), bf16[512,256]{1,0:T(8,128)(2,1)}) %reduce-scatter.32.cloned.1.call-update) | async-done | bytes 262160 | tf_op jit(solution)/shard_map/reduce_scatter | solution.py:332
  1297.6 77.3 %reduce-scatter.22.cloned.1.call-done = f32[128,2048]{1,0:T(8,128)} async-done(((f32[512,2048]{1,0:T(8,128)}), f32[128,2048]{1,0:T(8,128)}) %reduce-scatter.22.cloned.1.call-update) | async-done | bytes 1048592 | tf_op jit(solution)/shard_map/reduce_scatter | solution.py:161
  1376.4 18.8 %all-reduce.36 = (bf16[2048]{0:T(1024)(128)(2,1)S(1)}, f32[128]{0:T(128)S(1)}, bf16[2048]{0:T(1024)(128)(2,1)S(1)}) all-reduce(f32[2048]{0:T(1024)S(1)} %get-tuple-element.717, f32[128]{0:T(128)S(1)} %copy-done.109, f32[2048]{0:T(1024)S(1)} %get-tuple-element.701), channel_id=1, replica_groups=mesh['dp'=4,'fsdp'=2,'tensor'=4] {'tensor'}, use_global_device_ids=true, to_apply=%region_23.26 | all-reduce | flops 4224 | bytes 25600 | tf_op jit(solution)/shard_map/psum | solution.py:309
  1395.2 14.7 %all-reduce.37 = (bf16[2048]{0:T(1024)(128)(2,1)S(1)}, bf16[2048]{0:T(1024)(128)(2,1)S(1)}) all-reduce(bf16[2048]{0:T(1024)(128)(2,1)S(1)} %get-tuple-element.791, bf16[2048]{0:T(1024)(128)(2,1)S(1)} %get-tuple-element.793), channel_id=6, replica_groups=mesh['dp'=4,'fsdp'=2,'tensor'=4] {'dp','fsdp'}, use_global_device_ids=true, to_apply=%region_24.27.clone | all-reduce | flops 4096 | bytes 16384
  1409.9 24.7 %all-reduce.35 = (f32[4,512]{1,0:T(4,128)}, f32[4,512]{1,0:T(4,128)}, f32[4,512]{1,0:T(4,128)}, f32[128]{0:T(128)}) all-reduce(f32[4,512]{1,0:T(4,128)S(1)} %pad_add_fusion.2, f32[4,512]{1,0:T(4,128)S(1)} %pad_add_fusion.1, f32[4,512]{1,0:T(4,128)S(1)} %pad_add_fusion, ...), channel_id=1, replica_groups=mesh['dp'=4,'fsdp'=2,'tensor'=4] {'dp','fsdp'}, use_global_device_ids=true, to_apply=%region_34.37 | all-reduce | flops 6272 | bytes 50176 | tf_op jit(solution)/shard_map/psum | solution.py:310
  1435.8 19.3 %reduce-scatter.18.cloned.1.call-done = f32[128,2048]{1,0:T(8,128)} async-done(((f32[512,2048]{1,0:T(8,128)}), f32[128,2048]{1,0:T(8,128)}) %reduce-scatter.18.cloned.1.call-update) | async-done | bytes 1048592 | tf_op jit(solution)/shard_map/reduce_scatter | solution.py:161
  (609 shorter events, 462.6 us)
Async XLA Ops:
  7.2 72.7 %all-gather.13.cloned.1.call-start = ((), (), s32[]{:S(2)}) async-start(), calls=%async_computation.15 | async-start | bytes 3145728 | tf_op jit(solution)/shard_map/all_gather | solution.py:167
  7.9 75.8 %all-gather.11.cloned.1.call-start = ((), (), s32[]{:S(2)}) async-start(), calls=%async_computation.14 | async-start | bytes 3145728 | tf_op jit(solution)/shard_map/all_gather | solution.py:169
  8.7 106.3 %all-gather.9.cloned.1.call-start = ((), (), s32[]{:S(2)}) async-start(), calls=%async_computation.13 | async-start | bytes 3145728 | tf_op jit(solution)/shard_map/all_gather | solution.py:168
  9.5 371.4 %all-gather.15.cloned.1.call-start = ((), (), s32[]{:S(2)}) async-start(), calls=%async_computation.16 | async-start | bytes 3145728 | tf_op jit(solution)/shard_map/all_gather | solution.py:170
  10.0 376.8 %all-gather.17.cloned.1.call-start = ((), (), s32[]{:S(2)}) async-start(), calls=%async_computation.17 | async-start | bytes 3145728 | tf_op jit(solution)/shard_map/all_gather | solution.py:172
  16.0 12.9 collective-permute-start
  18.1 450.8 %reduce-scatter.16.cloned.1.call-start = ((), (), s32[]{:S(2)}) async-start(), calls=%async_computation.18 | async-start | bytes 5242880 | tf_op jit(solution)/shard_map/reduce_scatter | solution.py:161
  20.3 361.1 %copy-start.70 = (f32[512]{0:T(512)}, f32[512]{0:T(512)S(1)}, u32[]{:S(2)}) copy-start(f32[512]{0:T(512)S(1)} %fusion.167) | copy-start | bytes 6148
  29.1 46.8 %collective-permute-start.1 = (bf16[256,2048]{1,0:T(8,128)(2,1)S(1)}, bf16[256,2048]{1,0:T(8,128)(2,1)}, u32[]{:S(2)}, u32[]{:S(2)}) collective-permute-start(bf16[256,2048]{1,0:T(8,128)(2,1)S(1)} %maximum_select_fusion.4), channel_id=1, source_target_pairs={{0,2},{1,3},{2,0},{3,1},{4,6},{5,7},{6,4},{7,5},{8,10},{9,11},{10,... | collective-permute-start | bytes 3145736 | tf_op jit(solution)/shard_map/ppermute | solution.py:14
  391.9 153.6 %all-gather.19.cloned.1.call-start = ((), (), s32[]{:S(2)}) async-start(), calls=%async_computation.19 | async-start | bytes 8650752 | tf_op jit(solution)/shard_map/all_gather | solution.py:179
  392.7 229.0 %all-gather.21.cloned.1.call-start = ((), (), s32[]{:S(2)}) async-start(), calls=%async_computation.20 | async-start | bytes 8650752 | tf_op jit(solution)/shard_map/all_gather | solution.py:180
  393.4 304.3 %all-gather.23.cloned.1.call-start = ((), (), s32[]{:S(2)}) async-start(), calls=%async_computation.21 | async-start | bytes 8650752 | tf_op jit(solution)/shard_map/all_gather | solution.py:181
  394.1 403.3 %reduce-scatter.20.cloned.1.call-start = ((), (), s32[]{:S(2)}) async-start(), calls=%async_computation.23 | async-start | bytes 5242880 | tf_op jit(solution)/shard_map/reduce_scatter | solution.py:161
  470.5 328.6 %copy-start.97 = (f32[128]{0:T(128)}, f32[128]{0:T(128)S(1)}, u32[]{:S(2)}) copy-start(f32[128]{0:T(128)S(1)} %add_rsqrt_fusion.2) | copy-start | bytes 1540
  470.7 13.8 collective-permute-start.2
  485.8 71.3 %collective-permute-start.3 = (bf16[256,2048]{1,0:T(8,128)(2,1)}, bf16[256,2048]{1,0:T(8,128)(2,1)}, u32[]{:S(2)}, u32[]{:S(2)}) collective-permute-start(bf16[256,2048]{1,0:T(8,128)(2,1)} %maximum_select_fusion.5), channel_id=1, source_target_pairs={{0,2},{1,3},{2,0},{3,1},{4,6},{5,7},{6,4},{7,5},{8,10},{9,11},{10,... | collective-permute-start | bytes 3145736 | tf_op jit(solution)/shard_map/ppermute | solution.py:14
  488.7 33.1 %collective-permute-start.4 = (bf16[128,2048]{1,0:T(8,128)(2,1)S(1)}, bf16[128,2048]{1,0:T(8,128)(2,1)S(1)}, u32[]{:S(2)}, u32[]{:S(2)}) collective-permute-start(bf16[128,2048]{1,0:T(8,128)(2,1)S(1)} %copy-done.22), channel_id=1, source_target_pairs={{0,1},{1,0},{2,3},{3,2},{4,5},{5,4},{6,7},{7,6},{8,9},{9,8},{10,11... | collective-permute-start | bytes 1572872 | tf_op jit(solution)/shard_map/ppermute | solution.py:14
  523.0 107.6 %collective-permute-start.5 = (bf16[256,2048]{1,0:T(8,128)(2,1)}, bf16[256,2048]{1,0:T(8,128)(2,1)}, u32[]{:S(2)}, u32[]{:S(2)}) collective-permute-start(bf16[256,2048]{1,0:T(8,128)(2,1)} %maximum_select_fusion.6), channel_id=1, source_target_pairs={{0,2},{1,3},{2,0},{3,1},{4,6},{5,7},{6,4},{7,5},{8,10},{9,11},{10,... | collective-permute-start | bytes 3145736 | tf_op jit(solution)/shard_map/ppermute | solution.py:14
  720.6 382.1 %reduce-scatter.34.cloned.1.call-start = ((), (), s32[]{:S(2)}) async-start(), calls=%async_computation.30 | async-start | bytes 6488064 | tf_op jit(solution)/shard_map/reduce_scatter | solution.py:338
  729.5 375.4 %reduce-scatter.36.cloned.1.call-start = ((), (), s32[]{:S(2)}) async-start(), calls=%async_computation.31 | async-start | bytes 6488064 | tf_op jit(solution)/shard_map/reduce_scatter | solution.py:341
  738.3 369.0 %reduce-scatter.38.cloned.1.call-start = ((), (), s32[]{:S(2)}) async-start(), calls=%async_computation.32 | async-start | bytes 6488064 | tf_op jit(solution)/shard_map/reduce_scatter | solution.py:344
  799.5 13.8 collective-permute-start.6
  814.6 48.1 %collective-permute-start.7 = (bf16[256,2048]{1,0:T(8,128)(2,1)}, bf16[256,2048]{1,0:T(8,128)(2,1)}, u32[]{:S(2)}, u32[]{:S(2)}) collective-permute-start(bf16[256,2048]{1,0:T(8,128)(2,1)} %maximum_select_fusion.7), channel_id=1, source_target_pairs={{0,2},{1,3},{2,0},{3,1},{4,6},{5,7},{6,4},{7,5},{8,10},{9,11},{10,... | collective-permute-start | bytes 3145736 | tf_op jit(solution)/shard_map/ppermute | solution.py:14
  830.9 278.8 %reduce-scatter.40.cloned.1.call-start = ((), (), s32[]{:S(2)}) async-start(), calls=%async_computation.33 | async-start | bytes 589824
  1038.6 78.8 %reduce-scatter.24.cloned.1.call-start = ((), (), s32[]{:S(2)}) async-start(), calls=%async_computation.25 | async-start | bytes 2359296 | tf_op jit(solution)/shard_map/reduce_scatter | solution.py:317
  1055.9 106.3 %reduce-scatter.26.cloned.1.call-start = ((), (), s32[]{:S(2)}) async-start(), calls=%async_computation.26 | async-start | bytes 2359296 | tf_op jit(solution)/shard_map/reduce_scatter | solution.py:320
  1062.7 143.9 %reduce-scatter.28.cloned.1.call-start = ((), (), s32[]{:S(2)}) async-start(), calls=%async_computation.27 | async-start | bytes 2359296 | tf_op jit(solution)/shard_map/reduce_scatter | solution.py:323
  1069.5 181.8 %reduce-scatter.30.cloned.1.call-start = ((), (), s32[]{:S(2)}) async-start(), calls=%async_computation.28 | async-start | bytes 2359296 | tf_op jit(solution)/shard_map/reduce_scatter | solution.py:326
  1073.2 222.6 %reduce-scatter.32.cloned.1.call-start = ((), (), s32[]{:S(2)}) async-start(), calls=%async_computation.29 | async-start | bytes 2359296 | tf_op jit(solution)/shard_map/reduce_scatter | solution.py:332
  1079.3 295.6 %reduce-scatter.22.cloned.1.call-start = ((), (), s32[]{:S(2)}) async-start(), calls=%async_computation.24 | async-start | bytes 5242880 | tf_op jit(solution)/shard_map/reduce_scatter | solution.py:161
  1091.9 363.2 %reduce-scatter.18.cloned.1.call-start = ((), (), s32[]{:S(2)}) async-start(), calls=%async_computation.22 | async-start | bytes 5242880 | tf_op jit(solution)/shard_map/reduce_scatter | solution.py:161
  1164.0 291.1 %copy-start.98 = (f32[128]{0:T(128)S(1)}, f32[128]{0:T(128)}, u32[]{:S(2)}) copy-start(f32[128]{0:T(128)} %copy-done.97) | copy-start | bytes 1540
  (116 other events, 3520.2 us)
Sparse Core Ops, SparseCore 0:
  9.6 35.9 all-gather.12
  47.2 33.1 all-gather.10
  81.9 33.1 all-gather.8
  116.4 33.2 all-gather.14
  151.1 33.2 all-gather.16
  392.0 76.8 reduce-scatter.15
  470.5 74.9 all-gather.18
  547.1 74.4 all-gather.20
  623.2 74.4 all-gather.22
  720.7 76.7 reduce-scatter.19
  800.9 59.5 reduce-scatter.33
  864.2 58.9 reduce-scatter.35
  926.7 59.0 reduce-scatter.37
  1038.8 34.2 reduce-scatter.39
  1076.2 41.1 reduce-scatter.23
  1120.9 41.2 reduce-scatter.25
  1165.3 41.1 reduce-scatter.27
  1210.0 41.2 reduce-scatter.29
  1254.6 41.2 reduce-scatter.31
  1298.1 76.7 reduce-scatter.21
  1377.2 77.8 reduce-scatter.17
